TPU v7x, 32 devices: a whole 2x2x4 slice. The times are simulated.
32 devices in a mesh: store: 8 (over y, x, core), tp: 4 (over z).
Axes of the slice: x: 2, y: 2, z: 4, core: 2. Of those that a mesh axis runs over, the one named last changes fastest.
Arguments:
- hidden: bfloat16 [8, 576, 8192], P('store', None, 'tp'), may hold values from -300 to 300
- w_query: bfloat16 [8192, 4096], P(None, 'tp'), may hold values from -0.0625 to 0.0625
- w_keyvalue: bfloat16 [8192, 1024], P('tp'), may hold values from -0.1875 to 0.1875
- passage_cache: bfloat16 [32, 4, 384, 256], P('store'), may hold values from -400 to 400
- passage_ids: int32 [8, 8], replicated, may hold values from 0 to 31, as said below
- select_index: int32 [8, 576], P('store'), may hold values from 0 to 3071, as said below
- select_count: int32 [8], P('store'), may hold values from 288 to 576, as said below
Outputs:
- context: bfloat16 [8, 576, 4096], P('store', None, 'tp')
Inputs may be any that keep to these rules, and one draw needn't show every extreme that they name: `passage_ids`: the passages of one prompt lie in distinct shards of the pool, shard = id // 4. `select_index`: all entries of a row are distinct positions of the prompt; the first select_count[p] of row p are in increasing order, the others are ignored. `select_count`: some prompt of every draw has 576 selected tokens.
All inputs are finite; a program needn't handle non-finite values.
Results may differ from a plain program's by a relative error of at most 0.04.
Values may be sent and summed in bfloat16 or wider, within the bound.
No kernel may reach another device: no remote copies, remote signals or barrier semaphores. Data moves between devices by JAX's collectives and lax.ppermute only.
A program may use at most 128 MiB of HBM per device.

v0:
```python
import jax
import jax.numpy as jnp
from jax import lax
from jax.sharding import PartitionSpec as P

D = 8192
KV_HEADS = 4
HEAD_DIM = 128
PASSAGE = 384
PASSAGES = 8
SEQ = 3072
ROPE_BASE = 1000000.0
EPSILON = 1e-06


def rotate(vectors, positions):
    half_dim = vectors.shape[-1] // 2
    frequency = ROPE_BASE ** (-(jnp.arange(half_dim, dtype=jnp.float32) * 2.0) / vectors.shape[-1])
    angles = positions.astype(jnp.float32)[..., None] * frequency
    cosine = jnp.cos(angles)
    sine_part = jnp.sin(angles)
    front_half = vectors[..., :half_dim]
    back_half = vectors[..., half_dim:]
    return jnp.concatenate(
        [front_half * cosine - back_half * sine_part, back_half * cosine + front_half * sine_part],
        axis=-1,
    )


def local(hidden, w_query, w_keyvalue, passage_cache, passage_ids, select_index, select_count):
    tp_count = lax.axis_size("tp")
    group_width = tp_count // KV_HEADS
    tp_rank = lax.axis_index("tp")
    kv_head = tp_rank // group_width
    store_rank = lax.axis_index("store")
    local_heads = w_query.shape[1] // HEAD_DIM
    row_count = hidden.shape[1]
    pool_dev = passage_cache.shape[0]
    partial_kv = jnp.dot(hidden[0], w_keyvalue, preferred_element_type=jnp.float32)
    proj_kv = lax.psum(partial_kv, "tp")
    head_kv = lax.dynamic_slice_in_dim(proj_kv, kv_head * 2 * HEAD_DIM, 2 * HEAD_DIM, 1)
    token_part = lax.all_gather(hidden, "tp", axis=2, tiled=True)[0]
    widened = token_part.astype(jnp.float32)
    running = jnp.dot(token_part, w_query, preferred_element_type=jnp.float32)
    squares = jnp.sum(widened * widened, axis=-1)
    inverse_rms = lax.rsqrt(squares / D + EPSILON)
    positions = select_index[0]
    live_count = select_count[0]
    queries = rotate(
        (running * inverse_rms[:, None]).reshape(row_count, local_heads, HEAD_DIM),
        positions[:, None],
    )
    queries = (queries * HEAD_DIM ** (-0.5)).astype(jnp.bfloat16)
    key_value = head_kv * inverse_rms[:, None]
    new_keys = rotate(key_value[:, :HEAD_DIM], positions).astype(jnp.bfloat16)
    new_values = key_value[:, HEAD_DIM:].astype(jnp.bfloat16)
    head_cache = lax.dynamic_index_in_dim(passage_cache, kv_head, 1, keepdims=False)
    owners = passage_ids // pool_dev
    local_index = passage_ids % pool_dev
    matches = owners == store_rank
    local_slot = jnp.sum(jnp.where(matches, local_index, 0), axis=1)
    present = jnp.any(matches, axis=1)
    outgoing = jnp.take(head_cache, local_slot, axis=0) * present[:, None, None].astype(
        jnp.bfloat16
    )
    incoming = lax.all_to_all(outgoing, "store", split_axis=0, concat_axis=0, tiled=True)
    my_owners = lax.dynamic_index_in_dim(owners, store_rank, 0, keepdims=False)
    fetched = jnp.take(incoming, my_owners, axis=0)
    offsets = jnp.arange(PASSAGES) * PASSAGE
    old_keys = rotate(fetched[..., :HEAD_DIM].astype(jnp.float32), offsets[:, None]).astype(
        jnp.bfloat16
    )
    old_keys = old_keys.reshape(SEQ, HEAD_DIM)
    old_values = fetched[..., HEAD_DIM:].reshape(SEQ, HEAD_DIM)
    row_ids = jnp.arange(row_count, dtype=jnp.int32)
    target = jnp.where(row_ids < live_count, positions, SEQ)
    all_keys = old_keys.at[target].set(new_keys, mode="drop")
    all_values = old_values.at[target].set(new_values, mode="drop")
    allowed = jnp.arange(SEQ, dtype=jnp.int32)[None, :] <= positions[:, None]
    scores = jnp.einsum("rgd,sd->grs", queries, all_keys, preferred_element_type=jnp.float32)
    scores = jnp.where(allowed[None], scores, -jnp.inf)
    row_max = jnp.max(scores, axis=-1, keepdims=True)
    shifted = jnp.exp(scores - row_max)
    weight = (shifted / jnp.sum(shifted, axis=-1, keepdims=True)).astype(jnp.bfloat16)
    context = jnp.einsum("grs,sd->rgd", weight, all_values, preferred_element_type=jnp.float32)
    row_live = (row_ids < live_count)[:, None, None]
    context = jnp.where(row_live, context, 0.0)
    return context.reshape(1, row_count, local_heads * HEAD_DIM).astype(jnp.bfloat16)


def solution(mesh):
    in_specs = (
        P("store", None, "tp"),
        P(None, "tp"),
        P("tp", None),
        P("store", None, None, None),
        P(),
        P("store", None),
        P("store"),
    )
    out_specs = P("store", None, "tp")
    return jax.shard_map(local, mesh=mesh, in_specs=in_specs, out_specs=out_specs, check_vma=False)
```

profile of v0, /device:TPU:0, one launch (start us, length us, event | category | flops | bytes accessed | tf_op | source)
XLA Modules:
  0.0 357.8 jit_solution(9565624965004974671)
XLA Ops:
  6.5 0.0 copy-start
  6.5 0.0 copy-start.5
  6.5 0.0 all-gather.2.cloned.1.call-start
  6.5 0.7 all-gather.2.cloned.1.call-update
  7.3 0.1 copy-done.5
  7.4 0.1 fusion.36
  7.5 0.1 fusion.29
  7.6 0.8 copy-done
  8.4 0.9 dynamic-slice_bitcast_fusion
  9.4 1.8 gather_fusion
  11.2 1.3 select_multiply_fusion
  12.5 5.2 %all-to-all-start = ((bf16[8,384,256]{2,1,0:T(8,128)(2,1)}), bf16[8,384,256]{2,1,0:T(8,128)(2,1)S(1)}, u32[]{:S(2)}, u32[]{:S(2)}) async-start(bf16[8,384,256]{2,1,0:T(8,128)(2,1)} %select_multiply_fusion), calls=%async_computation | async-start | bytes 3145728 | tf_op jit(solution)/shard_map/all_to_all | solution.py:66
  17.7 0.0 all-reduce.2.cloned.1.call-start
  17.8 7.9 %fusion.10 = f32[576,1024]{1,0:T(8,128)} fusion(bf16[2048,1024]{1,0:T(8,128)(2,1)} %param.9, bf16[1,576,2048]{2,1,0:T(8,128)(2,1)} %param.7), kind=kOutput, calls=%fused_computation.19 | convolution fusion | flops 2415919104 | bytes 8912896 | tf_op jit(solution)/shard_map/dot_general | solution.py:39
  25.7 0.0 copy-start.6
  25.7 0.0 all-reduce.2.cloned.1.call-update
  26.4 0.0 copy-done.6
  26.5 0.1 multiply_cosine_fusion.1
  26.7 2.6 iota_compare_fusion
  29.2 9.5 %all-to-all-done = bf16[8,384,256]{2,1,0:T(8,128)(2,1)S(1)} async-done(((bf16[8,384,256]{2,1,0:T(8,128)(2,1)}), bf16[8,384,256]{2,1,0:T(8,128)(2,1)S(1)}, u32[]{:S(2)}, u32[]{:S(2)}) %all-to-all-start) | async-done | bytes 1572896 | tf_op jit(solution)/shard_map/all_to_all | solution.py:66
  38.7 1.8 gather_fusion.1
  40.5 1.6 broadcast_select_fusion
  42.1 1.1 fusion.38
  43.3 0.6 subtract_convert_fusion
  43.9 1.3 pad_maximum_fusion
  45.2 133.2 %all-gather.2.cloned.1.call-done = bf16[1,576,8192]{2,1,0:T(8,128)(2,1)} async-done(((bf16[1,576,2048]{2,1,0:T(8,128)(2,1)}), bf16[1,576,8192]{2,1,0:T(8,128)(2,1)}) %all-gather.2.cloned.1.call-update) | async-done | bytes 9437200 | tf_op jit(solution)/shard_map/all_gather | solution.py:42
  178.4 0.0 copy-start.2
  178.4 5.8 %multiply_reduce_fusion = f32[576]{0:T(1024)S(1)} fusion(bf16[1,576,8192]{2,1,0:T(8,128)(2,1)} %all-gather.2.cloned.1.call-done), kind=kLoop, calls=%fused_computation.12 | loop fusion | flops 14155200 | bytes 9439488 | tf_op jit(solution)/shard_map/reduce_sum | solution.py:45
  184.2 0.9 copy-done.2
  185.1 13.6 %multiply_bitcast_fusion = f32[72,8,8,128]{3,1,2,0:T(8,128)S(1)} fusion(bf16[8192,1024]{1,0:T(8,128)(2,1)} %param.8, bf16[1,576,8192]{2,1,0:T(8,128)(2,1)S(1)} %copy-done.2, f32[576]{0:T(1024)S(1)} %add_rsqrt_fusion), kind=kOutput, calls=%fused_computation.24 | convolution fusion | flops 9664266240 | bytes 28576000 | tf_op jit(solution)/shard_map/dot_general | solution.py:44
  198.7 0.5 copy.15
  199.2 2.9 fusion.37
  202.1 0.0 copy-start.3
  202.1 71.5 %all-reduce.2.cloned.1.call-done = f32[576,1024]{1,0:T(8,128)} async-done(((f32[576,1024]{1,0:T(8,128)}), f32[576,1024]{1,0:T(8,128)}) %all-reduce.2.cloned.1.call-update) | async-done | bytes 2359312 | tf_op jit(solution)/shard_map/psum | solution.py:40
  273.6 1.2 dynamic-slice_multiply_fusion
  274.9 2.1 subtract_convert_fusion.1
  276.9 6.4 %scatter_custom_fusion = bf16[3072,128]{1,0:T(8,128)(2,1)} fusion(bf16[3072,128]{1,0:T(8,128)(2,1)} %bitcast.68, s32[576]{0:T(1024)S(1)} %fusion.32, f32[576,256]{1,0:T(8,128)S(1)} %dynamic-slice_multiply_fusion), kind=kCustom, calls=%fused_computation.43 | custom fusion | bytes 933888 | tf_op jit(solution)/shard_map/scatter | solution.py:78
  283.3 7.2 %scatter_custom_fusion.1 = bf16[3072,128]{1,0:T(8,128)(2,1)} fusion(bf16[3072,128]{1,0:T(8,128)(2,1)} %pad_maximum_fusion, s32[576]{0:T(1024)S(1)} %fusion.32, bf16[576,64]{1,0:T(8,128)(2,1)} %get-tuple-element.17, bf16[]{:T(256)} %constant.123, bf16[576,64]{1,0:T(8,128)(2,1)S(1)} %get-tuple-element.16), kind=kCustom, calls=%fused_computation.44 | custom fusion | flops 294912 | bytes 1081856 | tf_op jit(solution)/shard_map/scatter | solution.py:77
  290.5 0.0 copy-done.3
  290.5 0.0 copy-start.4
  290.5 4.7 %multiply_subtract_fusion = (f32[576,8,64]{2,0,1:T(8,128)}, f32[576,8,64]{2,0,1:T(8,128)}) fusion(f32[576,8,64]{2,1,0:T(8,128)} %get-tuple-element.11, f32[576,8,64]{2,1,0:T(8,128)S(1)} %copy-done.3, f32[576,64]{1,0:T(8,128)S(1)} %get-tuple-element.18, f32[576,64]{1,0:T(8,128)} %get-tuple-element.19), kind=kLoop, calls=%fused_computation.23 | loop fusion | flops 1769472 | bytes 5013504 | tf_op jit(solution)/shard_map/sub | solution.py:25
  295.2 0.0 copy-done.4
  295.2 28.2 %fusion.39 = (f32[8,576]{1,0:T(8,128)S(1)}, f32[8,576,3072]{2,1,0:T(8,128)}) fusion(pred[576,3072]{1,0:T(8,128)(4,1)} %iota_compare_fusion, bf16[3072,128]{1,0:T(8,128)(2,1)S(1)} %copy-done.4, f32[576,8,64]{2,0,1:T(8,128)} %get-tuple-element.9, f32[576,8,64]{2,0,1:T(8,128)} %get-tuple-element.8), kind=kOutput, calls=%fused_computation.83 | convolution fusion | flops 3668118528 | bytes 61556736 | tf_op jit(solution)/shard_map/sub | solution.py:83
  323.4 0.0 copy-start.1
  323.4 21.4 %fusion.14 = bf16[576,8,128]{2,0,1:T(8,128)(2,1)} fusion(f32[8,576,3072]{2,1,0:T(8,128)} %get-tuple-element.23, f32[8,576]{1,0:T(8,128)S(1)} %get-tuple-element.22, pred[576]{0:T(1024)(128)(4,1)S(1)} %iota_compare_fusion.1, bf16[3072,128]{1,0:T(8,128)(2,1)} %scatter_custom_fusion), kind=kOutput, calls=%fused_computation.29 | convolution fusion | flops 3653369856 | bytes 58608192 | tf_op jit(solution)/shard_map/grs,sd->rgd/dot_general | solution.py:85
  344.9 3.0 copy.12
  347.9 3.0 convert_element_type.79
  351.0 0.0 copy-done.1
  (14 shorter events, 0.1 us)
Async XLA Ops:
  6.5 1.9 copy-start
  6.5 0.8 copy-start.5
  6.5 171.9 %all-gather.2.cloned.1.call-start = ((), (), s32[]{:S(2)}) async-start(), calls=%async_computation.2 | async-start | bytes 11796480 | tf_op jit(solution)/shard_map/all_gather | solution.py:42
  12.5 26.2 %all-to-all-start = ((bf16[8,384,256]{2,1,0:T(8,128)(2,1)}), bf16[8,384,256]{2,1,0:T(8,128)(2,1)S(1)}, u32[]{:S(2)}, u32[]{:S(2)}) async-start(bf16[8,384,256]{2,1,0:T(8,128)(2,1)} %select_multiply_fusion), calls=%async_computation | async-start | bytes 3145728 | tf_op jit(solution)/shard_map/all_to_all | solution.py:66
  17.7 255.9 %all-reduce.2.cloned.1.call-start = ((), (), s32[]{:S(2)}) async-start(), calls=%async_computation.1 | async-start | bytes 4718592 | tf_op jit(solution)/shard_map/psum | solution.py:40
  25.7 0.7 copy-start.6
  178.4 6.6 %copy-start.2 = (bf16[1,576,8192]{2,1,0:T(8,128)(2,1)S(1)}, bf16[1,576,8192]{2,1,0:T(8,128)(2,1)}, u32[]{:S(2)}) copy-start(bf16[1,576,8192]{2,1,0:T(8,128)(2,1)} %all-gather.2.cloned.1.call-done) | copy-start | bytes 28311556
  202.1 88.4 %copy-start.3 = (f32[576,8,64]{2,1,0:T(8,128)S(1)}, f32[576,8,64]{2,1,0:T(8,128)}, u32[]{:S(2)}) copy-start(f32[576,8,64]{2,1,0:T(8,128)} %get-tuple-element.10) | copy-start | bytes 3538948
  290.5 4.7 %copy-start.4 = (bf16[3072,128]{1,0:T(8,128)(2,1)S(1)}, bf16[3072,128]{1,0:T(8,128)(2,1)}, u32[]{:S(2)}) copy-start(bf16[3072,128]{1,0:T(8,128)(2,1)} %scatter_custom_fusion.1) | copy-start | bytes 2359300
  323.4 27.5 %copy-start.1 = (bf16[4,4,384,256]{3,2,1,0:T(8,128)(2,1)S(1)}, bf16[4,4,384,256]{3,2,1,0:T(8,128)(2,1)}, u32[]{:S(2)}) copy-start(bf16[4,4,384,256]{3,2,1,0:T(8,128)(2,1)} %param.10) | copy-start | bytes 9437188
Sparse Core Ops, SparseCore 0:
  8.9 169.4 all-gather.1
  180.8 92.8 all-reduce.1
where the time goes:
time: 358 us
  waiting for transfers between devices  215 us (60%)
  matrix products  71.2 us (20%)
  other arithmetic  30 us (8%)
  local copies, waits for them, and re-layouts  22.3 us (6%)
  between operations  14.2 us (4%)
  starting transfers between devices  5.24 us (1%)
    all_gather x1, waiting for transfers between devices, local(): token_part = lax.all_gather(hidden, 'tp', axis=2, tiled=True)[0]  133 us
    psum x1, waiting for transfers between devices, local(): proj_kv = lax.psum(partial_kv, 'tp')  71.5 us
    sub x1, matrix products, local(): shifted = jnp.exp(scores - row_max)  28.2 us
    dot_general x1, matrix products, local(): jnp.einsum('grs,sd->rgd', weight, all_values, preferred_element_type=jnp....  21.4 us
    dot_general x1, matrix products, local(): running = jnp.dot(token_part, w_query, preferred_element_type=jnp.float32)  13.6 us
    all_to_all x1, waiting for transfers between devices, local(): lax.all_to_all(outgoing, 'store', split_axis=0, concat_axis=0, tiled=True)  9.47 us
    dot_general x1, matrix products, local(): jnp.dot(hidden[0], w_keyvalue, preferred_element_type=jnp.float32)  7.94 us
  transfers between devices with their start and end apart: 3, of which 3 were waited for; matrix products, arithmetic and copies ran while one was open for 12% of the time, Pallas kernels for 0%

commit v1 on v0

--- a/solution.py
+++ b/solution.py
@@ -37,7 +37,7 @@
     row_count = hidden.shape[1]
     pool_dev = passage_cache.shape[0]
     partial_kv = jnp.dot(hidden[0], w_keyvalue, preferred_element_type=jnp.float32)
-    proj_kv = lax.psum(partial_kv, "tp")
+    proj_kv = jnp.sum(lax.all_gather(partial_kv, "tp"), axis=0)
     head_kv = lax.dynamic_slice_in_dim(proj_kv, kv_head * 2 * HEAD_DIM, 2 * HEAD_DIM, 1)
     token_part = lax.all_gather(hidden, "tp", axis=2, tiled=True)[0]
     widened = token_part.astype(jnp.float32)

time: 358 us -> 436 us (1.22)
  waiting for transfers between devices: 215 us -> 286 us
  other arithmetic: 30 us -> 36.7 us
    all_gather x0 -> x1, waiting for transfers between devices: none -> 142 us  [local(): proj_kv = jnp.sum(lax.all_gather(partial_kv, 'tp'), axis=0)]
    psum x1 -> x0, waiting for transfers between devices: 71.5 us -> none  [local(): proj_kv = lax.psum(partial_kv, 'tp')]
    all_to_all x1, waiting for transfers between devices: 9.47 us -> 17.5 us  [local(): lax.all_to_all(outgoing, 'store', split_axis=0, concat_axis=0, tiled=True)]
    all_gather x1, waiting for transfers between devices: 133 us -> 126 us  [local(): token_part = lax.all_gather(hidden, 'tp', axis=2, tiled=True)[0]]
    reduce_sum x0 -> x1, other arithmetic: none -> 6.44 us  [local(): proj_kv = jnp.sum(lax.all_gather(partial_kv, 'tp'), axis=0)]
  transfers between devices with their start and end apart: 3 -> 3, of which waited for: 3 -> 3; matrix products, arithmetic and copies ran while one was open for 12% -> 10% of each run, Pallas kernels for 0% -> 0%
where the time goes in v1:
time: 436 us
  waiting for transfers between devices  286 us (66%)
  matrix products  70.7 us (16%)
  other arithmetic  36.7 us (8%)
  local copies, waits for them, and re-layouts  22.2 us (5%)
  between operations  14.2 us (3%)
  starting transfers between devices  5.48 us (1%)
    all_gather x1, waiting for transfers between devices, local(): proj_kv = jnp.sum(lax.all_gather(partial_kv, 'tp'), axis=0)  142 us
    all_gather x1, waiting for transfers between devices, local(): token_part = lax.all_gather(hidden, 'tp', axis=2, tiled=True)[0]  126 us
    sub x1, matrix products, local(): shifted = jnp.exp(scores - row_max)  28 us
    dot_general x1, matrix products, local(): jnp.einsum('grs,sd->rgd', weight, all_values, preferred_element_type=jnp....  21.4 us
    all_to_all x1, waiting for transfers between devices, local(): lax.all_to_all(outgoing, 'store', split_axis=0, concat_axis=0, tiled=True)  17.5 us
    dot_general x1, matrix products, local(): running = jnp.dot(token_part, w_query, preferred_element_type=jnp.float32)  14.2 us
  transfers between devices with their start and end apart: 3, of which 3 were waited for; matrix products, arithmetic and copies ran while one was open for 10% of the time, Pallas kernels for 0%

profile of v1, /device:TPU:0, one launch (start us, length us, event | category | flops | bytes accessed | tf_op | source)
XLA Modules:
  0.0 435.7 jit_solution(4381174869794242931)
XLA Ops:
  6.5 0.0 copy-start
  6.5 0.0 all-gather.4.cloned.1.call-start
  6.5 0.7 all-gather.4.cloned.1.call-update
  7.3 0.0 all-gather.6.cloned.1.call-start
  7.3 7.1 %fusion.10 = f32[576,1024]{1,0:T(8,128)} fusion(bf16[2048,1024]{1,0:T(8,128)(2,1)} %param.9, bf16[1,576,2048]{2,1,0:T(8,128)(2,1)} %param.7), kind=kOutput, calls=%fused_computation.19 | convolution fusion | flops 2415919104 | bytes 8912896 | tf_op jit(solution)/shard_map/dot_general | solution.py:39
  14.4 0.0 copy-start.5
  14.4 0.0 all-gather.6.cloned.1.call-update
  14.4 0.7 copy-done.5
  15.1 0.1 fusion.36
  15.2 0.1 fusion.29
  15.3 0.0 copy-done
  15.3 0.9 dynamic-slice_bitcast_fusion
  16.3 1.8 gather_fusion
  18.1 1.4 select_multiply_fusion
  19.5 0.0 copy-start.6
  19.5 5.4 %all-to-all-start = ((bf16[8,384,256]{2,1,0:T(8,128)(2,1)}), bf16[8,384,256]{2,1,0:T(8,128)(2,1)S(1)}, u32[]{:S(2)}, u32[]{:S(2)}) async-start(bf16[8,384,256]{2,1,0:T(8,128)(2,1)} %select_multiply_fusion), calls=%async_computation | async-start | bytes 3145728 | tf_op jit(solution)/shard_map/all_to_all | solution.py:66
  25.6 0.0 copy-done.6
  25.7 0.1 multiply_cosine_fusion.1
  25.8 2.6 iota_compare_fusion
  28.4 17.5 %all-to-all-done = bf16[8,384,256]{2,1,0:T(8,128)(2,1)S(1)} async-done(((bf16[8,384,256]{2,1,0:T(8,128)(2,1)}), bf16[8,384,256]{2,1,0:T(8,128)(2,1)S(1)}, u32[]{:S(2)}, u32[]{:S(2)}) %all-to-all-start) | async-done | bytes 1572896 | tf_op jit(solution)/shard_map/all_to_all | solution.py:66
  45.9 1.8 gather_fusion.1
  47.8 1.6 broadcast_select_fusion
  49.4 1.1 fusion.38
  50.5 0.6 subtract_convert_fusion
  51.1 1.3 pad_maximum_fusion
  52.5 126.0 %all-gather.4.cloned.1.call-done = bf16[1,576,8192]{2,1,0:T(8,128)(2,1)} async-done(((bf16[1,576,2048]{2,1,0:T(8,128)(2,1)}), bf16[1,576,8192]{2,1,0:T(8,128)(2,1)}) %all-gather.4.cloned.1.call-update) | async-done | bytes 9437200 | tf_op jit(solution)/shard_map/all_gather | solution.py:42
  178.4 0.0 copy-start.2
  178.4 5.8 %multiply_reduce_fusion = f32[576]{0:T(1024)S(1)} fusion(bf16[1,576,8192]{2,1,0:T(8,128)(2,1)} %all-gather.4.cloned.1.call-done), kind=kLoop, calls=%fused_computation.12 | loop fusion | flops 14155200 | bytes 9439488 | tf_op jit(solution)/shard_map/reduce_sum | solution.py:45
  184.2 0.7 copy-done.2
  184.9 14.2 %multiply_bitcast_fusion = f32[72,8,8,128]{3,1,2,0:T(8,128)S(1)} fusion(bf16[8192,1024]{1,0:T(8,128)(2,1)} %param.8, bf16[1,576,8192]{2,1,0:T(8,128)(2,1)S(1)} %copy-done.2, f32[576]{0:T(1024)S(1)} %add_rsqrt_fusion), kind=kOutput, calls=%fused_computation.24 | convolution fusion | flops 9664266240 | bytes 28576000 | tf_op jit(solution)/shard_map/dot_general | solution.py:44
  199.1 0.5 copy.15
  199.6 3.0 fusion.37
  202.6 142.3 %all-gather.6.cloned.1.call-done = f32[2304,1024]{1,0:T(8,128)} async-done(((f32[576,1024]{1,0:T(8,128)}), f32[2304,1024]{1,0:T(8,128)}) %all-gather.6.cloned.1.call-update) | async-done | bytes 9437200 | tf_op jit(solution)/shard_map/all_gather | solution.py:40
  345.0 6.4 %reduce_sum.40 = f32[576,1024]{1,0:T(8,128)} reduce(f32[4,576,1024]{2,1,0:T(8,128)} %bitcast.67, f32[]{:T(128)} %constant.105.clone.1), dimensions={0}, to_apply=%region_2.3 | reduce | flops 1769472 | bytes 11796484 | tf_op jit(solution)/shard_map/reduce_sum | solution.py:40
  351.4 0.0 copy-start.3
  351.4 1.4 dynamic-slice_multiply_fusion
  352.8 2.1 subtract_convert_fusion.1
  354.8 6.7 %scatter_custom_fusion = bf16[3072,128]{1,0:T(8,128)(2,1)} fusion(bf16[3072,128]{1,0:T(8,128)(2,1)} %bitcast.70, s32[576]{0:T(1024)S(1)} %fusion.32, f32[576,256]{1,0:T(8,128)S(1)} %dynamic-slice_multiply_fusion), kind=kCustom, calls=%fused_computation.43 | custom fusion | bytes 933888 | tf_op jit(solution)/shard_map/scatter | solution.py:78
  361.5 7.2 %scatter_custom_fusion.1 = bf16[3072,128]{1,0:T(8,128)(2,1)} fusion(bf16[3072,128]{1,0:T(8,128)(2,1)} %pad_maximum_fusion, s32[576]{0:T(1024)S(1)} %fusion.32, bf16[576,64]{1,0:T(8,128)(2,1)} %get-tuple-element.17, bf16[]{:T(256)} %constant.123, bf16[576,64]{1,0:T(8,128)(2,1)S(1)} %get-tuple-element.16), kind=kCustom, calls=%fused_computation.44 | custom fusion | flops 294912 | bytes 1081856 | tf_op jit(solution)/shard_map/scatter | solution.py:77
  368.6 0.0 copy-done.3
  368.6 0.0 copy-start.4
  368.6 4.7 %multiply_subtract_fusion = (f32[576,8,64]{2,0,1:T(8,128)}, f32[576,8,64]{2,0,1:T(8,128)}) fusion(f32[576,8,64]{2,1,0:T(8,128)} %get-tuple-element.11, f32[576,8,64]{2,1,0:T(8,128)S(1)} %copy-done.3, f32[576,64]{1,0:T(8,128)S(1)} %get-tuple-element.18, f32[576,64]{1,0:T(8,128)} %get-tuple-element.19), kind=kLoop, calls=%fused_computation.23 | loop fusion | flops 1769472 | bytes 5013504 | tf_op jit(solution)/shard_map/sub | solution.py:25
  373.4 0.0 copy-done.4
  373.4 28.0 %fusion.39 = (f32[8,576]{1,0:T(8,128)S(1)}, f32[8,576,3072]{2,1,0:T(8,128)}) fusion(pred[576,3072]{1,0:T(8,128)(4,1)} %iota_compare_fusion, bf16[3072,128]{1,0:T(8,128)(2,1)S(1)} %copy-done.4, f32[576,8,64]{2,0,1:T(8,128)} %get-tuple-element.9, f32[576,8,64]{2,0,1:T(8,128)} %get-tuple-element.8), kind=kOutput, calls=%fused_computation.83 | convolution fusion | flops 3668118528 | bytes 61556736 | tf_op jit(solution)/shard_map/sub | solution.py:83
  401.4 21.4 %fusion.14 = bf16[576,8,128]{2,0,1:T(8,128)(2,1)} fusion(f32[8,576,3072]{2,1,0:T(8,128)} %get-tuple-element.23, f32[8,576]{1,0:T(8,128)S(1)} %get-tuple-element.22, pred[576]{0:T(1024)(128)(4,1)S(1)} %iota_compare_fusion.1, bf16[3072,128]{1,0:T(8,128)(2,1)} %scatter_custom_fusion), kind=kOutput, calls=%fused_computation.29 | convolution fusion | flops 3653369856 | bytes 58608192 | tf_op jit(solution)/shard_map/grs,sd->rgd/dot_general | solution.py:85
  422.8 3.0 copy.12
  425.8 3.0 convert_element_type.79
  428.9 0.0 copy-done.1
  (15 shorter events, 0.1 us)
Async XLA Ops:
  6.5 8.8 %copy-start = (bf16[4,4,384,256]{3,2,1,0:T(8,128)(2,1)S(1)}, bf16[4,4,384,256]{3,2,1,0:T(8,128)(2,1)}, u32[]{:S(2)}) copy-start(bf16[4,4,384,256]{3,2,1,0:T(8,128)(2,1)} %param.10) | copy-start | bytes 9437188
  6.5 171.9 %all-gather.4.cloned.1.call-start = ((), (), s32[]{:S(2)}) async-start(), calls=%async_computation.1 | async-start | bytes 11796480 | tf_op jit(solution)/shard_map/all_gather | solution.py:42
  7.3 337.7 %all-gather.6.cloned.1.call-start = ((), (), s32[]{:S(2)}) async-start(), calls=%async_computation.2 | async-start | bytes 11796480 | tf_op jit(solution)/shard_map/all_gather | solution.py:40
  14.4 0.7 copy-start.5
  19.5 6.1 %copy-start.6 = (s32[1,576]{1,0:T(1,128)S(1)}, s32[1,576]{1,0:T(1,128)}, u32[]{:S(2)}) copy-start(s32[1,576]{1,0:T(1,128)} %param.12) | copy-start | bytes 6916
  19.5 26.4 %all-to-all-start = ((bf16[8,384,256]{2,1,0:T(8,128)(2,1)}), bf16[8,384,256]{2,1,0:T(8,128)(2,1)S(1)}, u32[]{:S(2)}, u32[]{:S(2)}) async-start(bf16[8,384,256]{2,1,0:T(8,128)(2,1)} %select_multiply_fusion), calls=%async_computation | async-start | bytes 3145728 | tf_op jit(solution)/shard_map/all_to_all | solution.py:66
  178.4 6.5 %copy-start.2 = (bf16[1,576,8192]{2,1,0:T(8,128)(2,1)S(1)}, bf16[1,576,8192]{2,1,0:T(8,128)(2,1)}, u32[]{:S(2)}) copy-start(bf16[1,576,8192]{2,1,0:T(8,128)(2,1)} %all-gather.4.cloned.1.call-done) | copy-start | bytes 28311556
  351.4 17.2 %copy-start.3 = (f32[576,8,64]{2,1,0:T(8,128)S(1)}, f32[576,8,64]{2,1,0:T(8,128)}, u32[]{:S(2)}) copy-start(f32[576,8,64]{2,1,0:T(8,128)} %get-tuple-element.10) | copy-start | bytes 3538948
  368.6 4.7 %copy-start.4 = (bf16[3072,128]{1,0:T(8,128)(2,1)S(1)}, bf16[3072,128]{1,0:T(8,128)(2,1)}, u32[]{:S(2)}) copy-start(bf16[3072,128]{1,0:T(8,128)(2,1)} %scatter_custom_fusion.1) | copy-start | bytes 2359300
  401.4 27.5 %copy-start.1 = (bf16[4,4,384,256]{3,2,1,0:T(8,128)(2,1)S(1)}, bf16[4,4,384,256]{3,2,1,0:T(8,128)(2,1)}, u32[]{:S(2)}) copy-start(bf16[4,4,384,256]{3,2,1,0:T(8,128)(2,1)} %param.10) | copy-start | bytes 9437188
Sparse Core Ops, SparseCore 0:
  8.9 169.4 all-gather.3
  180.0 164.9 all-gather.5
